TPU v7x, 512 devices: a whole 4x8x8 slice. The times are simulated.
512 devices in a mesh: row: 16 (over y, core), col: 32 (over z, x).
Axes of the slice: x: 4, y: 8, z: 8, core: 2. Of those that a mesh axis runs over, the one named last changes fastest.
Arguments:
- points: bfloat16 [128, 65536], P(None, ('row', 'col')), may hold values from -6 to 6
- inv_scale: float32 [128], replicated, may hold values from 0.07 to 0.22
- basis: bfloat16 [65536, 4096], P(('row', 'col')), may hold values from -0.25 to 0.25
- shrink: float32 [4096], replicated, may hold values from 0.02 to 1
- solution: float32 [33, 65536], P(None, ('row', 'col')), may hold values from -6 to 6
- residual: float32 [33, 65536], P(None, ('row', 'col')), may hold values from -6 to 6
- direction_prev: float32 [33, 65536], P(None, ('row', 'col')), may hold values from -6 to 6
- rz_prev: float32 [33], replicated, may hold values from 65536 to 262144
Outputs:
- solution_next: float32 [33, 65536], P(None, ('row', 'col'))
- residual_next: float32 [33, 65536], P(None, ('row', 'col'))
- direction: float32 [33, 65536], P(None, ('row', 'col'))
All inputs are finite; a program needn't handle non-finite values.
Results may differ from a plain program's by a relative error of at most 0.019.
Values may be sent and summed in bfloat16 or wider, within the bound.
A program may use at most 64 MiB of HBM per device.

v0:
```python
import jax
import jax.numpy as jnp
from jax import lax
from jax.sharding import PartitionSpec as P

noise_level = 0.25


def local(points, inv_scale, basis, shrink, solution, residual, direction_prev, rz_prev):
    scaled = (points * inv_scale[:, None]).astype(jnp.bfloat16)
    residual_bf = residual.astype(jnp.bfloat16)
    local_proj = jnp.dot(residual_bf, basis, preferred_element_type=jnp.float32)
    damping = shrink - 1.0
    projected = lax.psum(local_proj, ("row", "col"))
    correction = (damping[None, :] * projected).astype(jnp.bfloat16)
    precond = residual + jnp.dot(correction, basis.T, preferred_element_type=jnp.float32)
    precond_inner = lax.psum(jnp.sum(residual * precond, axis=1), ("row", "col"))
    direction = precond + (precond_inner / rz_prev)[:, None] * direction_prev
    direction_bf = direction.astype(jnp.bfloat16)
    row_points = lax.all_gather(scaled, "col", axis=1, tiled=True)
    row_sq = jnp.sum(jnp.square(row_points.astype(jnp.float32)), axis=0)
    rows_total = row_points.shape[1]
    width = min(1024, rows_total)
    direction_piece = lax.all_gather(direction_bf, "row", axis=1, tiled=True)
    column_pts = lax.all_gather(scaled, "row", axis=1, tiled=True)
    column_sq = jnp.sum(jnp.square(column_pts.astype(jnp.float32)), axis=0)
    results = []
    for offset in range(0, rows_total, width):
        rows = row_points[:, offset : offset + width]
        cross = lax.dot_general(
            column_pts, rows, (((0,), (0,)), ((), ())), preferred_element_type=jnp.float32
        )
        distance = jnp.maximum(
            column_sq[:, None] + row_sq[None, offset : offset + width] - 2.0 * cross, 0.0
        )
        tile = jnp.exp(-0.5 * distance).astype(jnp.bfloat16)
        results.append(jnp.dot(direction_piece, tile, preferred_element_type=jnp.float32))
    image_part = jnp.concatenate(results, axis=1)
    image = (
        lax.psum_scatter(
            image_part.astype(jnp.bfloat16), "col", scatter_dimension=1, tiled=True
        ).astype(jnp.float32)
        + noise_level * direction
    )
    curvature = lax.psum(jnp.sum(direction * image, axis=1), ("row", "col"))
    alpha = precond_inner / curvature
    solution_next = solution + alpha[:, None] * direction
    residual_next = residual - alpha[:, None] * image
    return (solution_next, residual_next, direction)


def solution(mesh):
    placed = (
        P(None, ("row", "col")),
        P(),
        P(("row", "col"), None),
        P(),
        P(None, ("row", "col")),
        P(None, ("row", "col")),
        P(None, ("row", "col")),
        P(),
    )
    return jax.shard_map(
        local,
        mesh=mesh,
        in_specs=placed,
        out_specs=(P(None, ("row", "col")), P(None, ("row", "col")), P(None, ("row", "col"))),
        check_vma=False,
    )
```

profile of v0, /device:TPU:1, one launch (start us, length us, event | category | flops | bytes accessed | tf_op | source)
XLA Modules:
  0.0 740.1 jit_solution(11344339179035116326)
XLA Ops:
  8.0 0.0 all-reduce.2.cloned.1.call-start
  8.1 1.2 copy-done
  9.2 1.9 fusion.17
  11.1 0.0 all-gather.2.cloned.1.call-start
  11.2 0.7 multiply_convert_fusion.2
  11.9 0.0 reduce-scatter.4.cloned.1.call-start
  11.9 22.7 %all_gather.10 = bf16[128,2048]{1,0:T(8,128)(2,1)S(1)} all-gather(bf16[128,128]{1,0:T(8,128)(2,1)} %multiply_convert_fusion.2), channel_id=1, replica_groups=mesh['row'=16,'col'=32] {'row'}, dimensions={1}, use_global_device_ids=true | all-gather | bytes 557056 | tf_op jit(solution)/shard_map/all_gather | solution.py:25
  34.6 0.1 multiply_reduce_fusion.1
  34.8 256.8 %all-reduce.2.cloned.1.call-done = f32[33,4096]{1,0:T(8,128)} async-done(((f32[33,4096]{1,0:T(8,128)}), f32[33,4096]{1,0:T(8,128)}) %all-reduce.2.cloned.1.call-update) | async-done | bytes 540688 | tf_op jit(solution)/shard_map/psum | solution.py:14
  291.6 1.7 multiply_reduce_fusion.3
  293.3 97.0 %psum.22 = f32[33]{0:T(128)S(1)} all-reduce(f32[33]{0:T(128)S(1)} %get-tuple-element.11), channel_id=1, replica_groups=mesh['row'=16,'col'=32] {'row','col'}, use_global_device_ids=true, to_apply=%region_2.0 | all-reduce | flops 33 | bytes 264 | tf_op jit(solution)/shard_map/psum | solution.py:17
  390.3 0.1 fusion.31
  390.4 15.4 %all_gather.9 = bf16[33,2048]{1,0:T(8,128)(2,1)S(1)} all-gather(bf16[33,128]{1,0:T(8,128)(2,1)S(1)} %get-tuple-element.3), channel_id=1, replica_groups=mesh['row'=16,'col'=32] {'row'}, dimensions={1}, use_global_device_ids=true | all-gather | bytes 143616 | tf_op jit(solution)/shard_map/all_gather | solution.py:24
  405.7 1.5 multiply_reduce_fusion
  407.3 2.7 fusion.4
  410.0 2.7 fusion.5
  412.7 2.7 fusion.6
  415.5 2.7 fusion.7
  418.2 1.4 copy.11
  419.7 210.6 %reduce-scatter.4.cloned.1.call-done = bf16[128,33]{1,0:T(8,128)(2,1)} async-done(((bf16[4096,33]{1,0:T(8,128)(2,1)}), bf16[128,33]{1,0:T(8,128)(2,1)}) %reduce-scatter.4.cloned.1.call-update) | async-done | bytes 8464
  630.3 0.8 copy.12
  631.1 0.1 multiply_reduce_fusion.2
  631.2 100.7 %psum.23 = f32[33]{0:T(128)S(1)} all-reduce(f32[33]{0:T(128)S(1)} %multiply_reduce_fusion.2), channel_id=1, replica_groups=mesh['row'=16,'col'=32] {'row','col'}, use_global_device_ids=true, to_apply=%region_7.0 | all-reduce | flops 33 | bytes 264 | tf_op jit(solution)/shard_map/psum | solution.py:45
  731.9 0.7 multiply_subtract_fusion
  (28 shorter events, 0.1 us)
Async XLA Ops:
  8.0 1.2 copy-start
  8.0 3.2 copy-start.4
  8.0 3.2 copy-start.8
  8.0 283.6 %all-reduce.2.cloned.1.call-start = ((), (), s32[]{:S(2)}) async-start(), calls=%async_computation.1 | async-start | bytes 1310720 | tf_op jit(solution)/shard_map/psum | solution.py:14
  11.1 23.7 %copy-start.7 = (f32[4096]{0:T(1024)S(1)}, f32[4096]{0:T(1024)}, u32[]{:S(2)}) copy-start(f32[4096]{0:T(1024)} %param.11) | copy-start | bytes 49156
  11.1 280.5 %copy-start.3 = (f32[33,128]{1,0:T(8,128)S(1)}, f32[33,128]{1,0:T(8,128)}, u32[]{:S(2)}) copy-start(f32[33,128]{1,0:T(8,128)} %param.13) | copy-start | bytes 50692
  11.1 394.6 %all-gather.2.cloned.1.call-start = ((), (), s32[]{:S(2)}) async-start(), calls=%async_computation.2 | async-start | bytes 1081344 | tf_op jit(solution)/shard_map/all_gather | solution.py:20
  11.9 618.4 %reduce-scatter.4.cloned.1.call-start = ((), (), s32[]{:S(2)}) async-start(), calls=%async_computation.3 | async-start | bytes 1081344
  34.6 355.6 %copy-start.9 = (f32[33]{0:T(128)S(1)}, f32[33]{0:T(128)}, u32[]{:S(2)}) copy-start(f32[33]{0:T(128)} %param.15) | copy-start | bytes 400
  34.6 355.6 %copy-start.6 = (f32[33,128]{1,0:T(8,128)S(1)}, f32[33,128]{1,0:T(8,128)}, u32[]{:S(2)}) copy-start(f32[33,128]{1,0:T(8,128)} %param.14) | copy-start | bytes 50692
  390.4 341.6 %copy-start.2 = (f32[33,128]{1,0:T(8,128)}, f32[33,128]{1,0:T(8,128)S(1)}, u32[]{:S(2)}) copy-start(f32[33,128]{1,0:T(8,128)S(1)} %get-tuple-element.4) | copy-start | bytes 50692
  405.7 1.6 copy-start.1
  418.2 313.7 %copy-start.5 = (f32[33,128]{1,0:T(8,128)S(1)}, f32[33,128]{1,0:T(8,128)}, u32[]{:S(2)}) copy-start(f32[33,128]{1,0:T(8,128)} %param.12) | copy-start | bytes 50692
Sparse Core Ops, SparseCore 0:
  13.8 277.7 all-reduce.1
Sparse Core Ops, SparseCore 1:
  15.1 78.6 all-gather.1
  419.7 210.5 reduce-scatter.3
where the time goes:
time: 740 us
  waiting for transfers between devices  467 us (63%)
  blocking collectives  236 us (32%)
  between operations  15.6 us (2%)
  matrix products  14.4 us (2%)
    psum x1, waiting for transfers between devices, local(): projected = lax.psum(local_proj, ('row', 'col'))  257 us
    unnamed x4, waiting for transfers between devices  211 us
    psum x1, blocking collectives, local(): curvature = lax.psum(jnp.sum(direction * image, axis=1), ('row', 'col'))  101 us
    psum x1, blocking collectives, local(): lax.psum(jnp.sum(residual * precond, axis=1), ('row', 'col'))  97 us
    all_gather x1, blocking collectives, local(): column_pts = lax.all_gather(scaled, 'row', axis=1, tiled=True)  22.7 us
    all_gather x1, blocking collectives, local(): direction_piece = lax.all_gather(direction_bf, 'row', axis=1, tiled=True)  15.4 us
  transfers between devices with their start and end apart: 3, of which 2 were waited for; matrix products, arithmetic and copies ran while one was open for 0% of the time, Pallas kernels for 0%

commit v1 on v0

--- a/solution.py
+++ b/solution.py
@@ -22,7 +22,9 @@
     rows_total = row_points.shape[1]
     width = min(1024, rows_total)
     direction_piece = lax.all_gather(direction_bf, "row", axis=1, tiled=True)
-    column_pts = lax.all_gather(scaled, "row", axis=1, tiled=True)
+    column_pts = jnp.concatenate(
+        lax.all_to_all(jnp.stack([scaled] * lax.axis_size("row")), "row", 0, 0), axis=1
+    )
     column_sq = jnp.sum(jnp.square(column_pts.astype(jnp.float32)), axis=0)
     results = []
     for offset in range(0, rows_total, width):

time: 740 us -> 741 us (level)
  blocking collectives: 236 us -> 213 us
  waiting for transfers between devices: 467 us -> 479 us
  starting transfers between devices: 0.13 us -> 10.4 us
    all_gather x1 -> x0, blocking collectives: 22.7 us -> none  [local(): column_pts = lax.all_gather(scaled, 'row', axis=1, tiled=True)]
    psum x1, waiting for transfers between devices: 257 us -> 268 us  [local(): projected = lax.psum(local_proj, ('row', 'col'))]
    all_to_all x0 -> x1, starting transfers between devices: none -> 10.2 us  [local(): lax.all_to_all(jnp.stack([scaled] * lax.axis_size('row')), 'row', 0, 0)]
  transfers between devices with their start and end apart: 3 -> 4, of which waited for: 2 -> 2; matrix products, arithmetic and copies ran while one was open for 0% -> 1% of each run, Pallas kernels for 0% -> 0%
where the time goes in v1:
time: 741 us
  waiting for transfers between devices  479 us (65%)
  blocking collectives  213 us (29%)
  between operations  15.7 us (2%)
  matrix products  13.8 us (2%)
  starting transfers between devices  10.4 us (1%)
    psum x1, waiting for transfers between devices, local(): projected = lax.psum(local_proj, ('row', 'col'))  268 us
    unnamed x4, waiting for transfers between devices  211 us
    psum x1, blocking collectives, local(): curvature = lax.psum(jnp.sum(direction * image, axis=1), ('row', 'col'))  101 us
    psum x1, blocking collectives, local(): lax.psum(jnp.sum(residual * precond, axis=1), ('row', 'col'))  97 us
    all_gather x1, blocking collectives, local(): direction_piece = lax.all_gather(direction_bf, 'row', axis=1, tiled=True)  15.4 us
  transfers between devices with their start and end apart: 4, of which 2 were waited for; matrix products, arithmetic and copies ran while one was open for 1% of the time, Pallas kernels for 0%

profile of v1, /device:TPU:1, one launch (start us, length us, event | category | flops | bytes accessed | tf_op | source)
XLA Modules:
  0.0 740.9 jit_solution(16758987094460423741)
XLA Ops:
  8.1 1.2 copy-done
  9.2 1.9 fusion.17
  11.2 0.7 multiply_convert_fusion.2
  11.9 0.9 copy.12
  12.8 0.9 stack.2
  13.7 10.2 %all-to-all-start = ((bf16[16,128,128]{1,2,0:T(8,128)(2,1)}), bf16[16,128,128]{1,2,0:T(8,128)(2,1)S(1)}, u32[]{:S(2)}, u32[]{:S(2)}) async-start(bf16[16,128,128]{1,2,0:T(8,128)(2,1)} %stack.2), calls=%async_computation | async-start | bytes 1048576 | tf_op jit(solution)/shard_map/all_to_all | solution.py:26
  24.0 0.0 reduce-scatter.4.cloned.1.call-start
  24.1 268.2 %all-reduce.2.cloned.1.call-done = f32[33,4096]{1,0:T(8,128)} async-done(((f32[33,4096]{1,0:T(8,128)}), f32[33,4096]{1,0:T(8,128)}) %all-reduce.2.cloned.1.call-update) | async-done | bytes 540688 | tf_op jit(solution)/shard_map/psum | solution.py:14
  292.2 1.7 multiply_reduce_fusion.3
  293.9 97.0 %psum.22 = f32[33]{0:T(128)S(1)} all-reduce(f32[33]{0:T(128)S(1)} %get-tuple-element.11), channel_id=1, replica_groups=mesh['row'=16,'col'=32] {'row','col'}, use_global_device_ids=true, to_apply=%region_2.0 | all-reduce | flops 33 | bytes 264 | tf_op jit(solution)/shard_map/psum | solution.py:17
  390.9 0.1 fusion.31
  391.0 15.4 %all_gather.6 = bf16[33,2048]{1,0:T(8,128)(2,1)S(1)} all-gather(bf16[33,128]{1,0:T(8,128)(2,1)S(1)} %get-tuple-element.3), channel_id=1, replica_groups=mesh['row'=16,'col'=32] {'row'}, dimensions={1}, use_global_device_ids=true | all-gather | bytes 143616 | tf_op jit(solution)/shard_map/all_gather | solution.py:24
  406.3 0.3 multiply_reduce_fusion.1
  406.7 1.5 multiply_reduce_fusion
  408.3 2.6 fusion.4
  410.9 2.6 fusion.5
  413.4 2.6 fusion.6
  416.0 2.6 fusion.7
  418.6 1.4 copy.13
  420.0 211.0 %reduce-scatter.4.cloned.1.call-done = bf16[128,33]{1,0:T(8,128)(2,1)} async-done(((bf16[4096,33]{1,0:T(8,128)(2,1)}), bf16[128,33]{1,0:T(8,128)(2,1)}) %reduce-scatter.4.cloned.1.call-update) | async-done | bytes 8464
  631.0 0.8 copy.14
  631.9 0.1 multiply_reduce_fusion.2
  632.0 100.7 %psum.23 = f32[33]{0:T(128)S(1)} all-reduce(f32[33]{0:T(128)S(1)} %multiply_reduce_fusion.2), channel_id=1, replica_groups=mesh['row'=16,'col'=32] {'row','col'}, use_global_device_ids=true, to_apply=%region_7.0 | all-reduce | flops 33 | bytes 264 | tf_op jit(solution)/shard_map/psum | solution.py:47
  732.7 0.7 multiply_subtract_fusion
  (31 shorter events, 0.3 us)
Async XLA Ops:
  8.0 1.2 copy-start
  8.0 3.2 copy-start.4
  8.0 3.2 copy-start.8
  8.0 284.2 %all-reduce.2.cloned.1.call-start = ((), (), s32[]{:S(2)}) async-start(), calls=%async_computation.2 | async-start | bytes 1310720 | tf_op jit(solution)/shard_map/psum | solution.py:14
  11.1 12.9 %copy-start.7 = (f32[4096]{0:T(1024)S(1)}, f32[4096]{0:T(1024)}, u32[]{:S(2)}) copy-start(f32[4096]{0:T(1024)} %param.11) | copy-start | bytes 49156
  11.1 281.1 %copy-start.3 = (f32[33,128]{1,0:T(8,128)S(1)}, f32[33,128]{1,0:T(8,128)}, u32[]{:S(2)}) copy-start(f32[33,128]{1,0:T(8,128)} %param.13) | copy-start | bytes 50692
  11.1 395.6 %all-gather.2.cloned.1.call-start = ((), (), s32[]{:S(2)}) async-start(), calls=%async_computation.3 | async-start | bytes 1081344 | tf_op jit(solution)/shard_map/all_gather | solution.py:20
  13.7 392.6 %all-to-all-start = ((bf16[16,128,128]{1,2,0:T(8,128)(2,1)}), bf16[16,128,128]{1,2,0:T(8,128)(2,1)S(1)}, u32[]{:S(2)}, u32[]{:S(2)}) async-start(bf16[16,128,128]{1,2,0:T(8,128)(2,1)} %stack.2), calls=%async_computation | async-start | bytes 1048576 | tf_op jit(solution)/shard_map/all_to_all | solution.py:26
  24.0 366.9 %copy-start.9 = (f32[33]{0:T(128)S(1)}, f32[33]{0:T(128)}, u32[]{:S(2)}) copy-start(f32[33]{0:T(128)} %param.15) | copy-start | bytes 400
  24.0 366.9 %copy-start.6 = (f32[33,128]{1,0:T(8,128)S(1)}, f32[33,128]{1,0:T(8,128)}, u32[]{:S(2)}) copy-start(f32[33,128]{1,0:T(8,128)} %param.14) | copy-start | bytes 50692
  24.0 607.1 %reduce-scatter.4.cloned.1.call-start = ((), (), s32[]{:S(2)}) async-start(), calls=%async_computation.4 | async-start | bytes 1081344
  391.0 341.7 %copy-start.2 = (f32[33,128]{1,0:T(8,128)}, f32[33,128]{1,0:T(8,128)S(1)}, u32[]{:S(2)}) copy-start(f32[33,128]{1,0:T(8,128)S(1)} %get-tuple-element.4) | copy-start | bytes 50692
  406.7 1.6 copy-start.1
  418.6 314.1 %copy-start.5 = (f32[33,128]{1,0:T(8,128)S(1)}, f32[33,128]{1,0:T(8,128)}, u32[]{:S(2)}) copy-start(f32[33,128]{1,0:T(8,128)} %param.12) | copy-start | bytes 50692
Sparse Core Ops, SparseCore 0:
  13.8 278.3 all-reduce.1
Sparse Core Ops, SparseCore 1:
  15.1 78.7 all-gather.1
  420.1 210.9 reduce-scatter.3
